TPU v7x, 32 devices: a whole 2x2x4 slice. The times are simulated.
32 devices in a mesh: role: 2 (over core), seq: 4 (over z), tp: 4 (over y, x).
Axes of the slice: x: 2, y: 2, z: 4, core: 2. Of those that a mesh axis runs over, the one named last changes fastest.
Arguments:
- merger_hidden: bfloat16 [512, 5120], P(('role', 'seq'), 'tp'), may hold values from -6 to 6
- merger_out: bfloat16 [5120, 8192], P('tp', ('role', 'seq')), may hold values from -0.078125 to 0.078125
- row_position: int32 [512], P(('role', 'seq')), may hold values from -1 to 2047, as said below
- prompt_embeds: bfloat16 [2048, 8192], P(('role', 'seq'), 'tp'), may hold values from -300 to 300
- norm_gain: bfloat16 [8192], P('tp'), may hold values from 0.099609375 to 1.8984375
- query_weight: bfloat16 [8192, 4096], P(None, 'tp'), may hold values from -2.762136 to 2.762136
- key_weight: bfloat16 [8192, 512], P(None, 'tp'), may hold values from -0.06629126 to 0.06629126
- value_weight: bfloat16 [8192, 512], P(None, 'tp'), may hold values from -0.0625 to 0.0625
Outputs:
- stream: bfloat16 [2048, 8192], P(('role', 'seq'), 'tp')
- context: bfloat16 [2048, 4096], P(('role', 'seq'), 'tp')
Inputs may be any that keep to these rules, and one draw needn't show every extreme that they name: `row_position`: the live slots of each device's 64 come first and hold distinct prompt positions, distinct over all devices; the other slots hold -1. Of one device's slots at most 16 hold positions of one owner's block (positions j * 256 to (j + 1) * 256 - 1); every device has 16 or more live slots.
All inputs are finite; a program needn't handle non-finite values.
Results may differ from a plain program's by a relative error of at most 0.012.
The roundings to bfloat16 on the way count: a program that leaves them out, or rounds other values in their place, can miss the bound.
Values may be sent and summed in bfloat16 or wider, within the bound.
No kernel may reach another device: no remote copies, remote signals or barrier semaphores. Data moves between devices by JAX's collectives and lax.ppermute only.
A program may use at most 192 MiB of HBM per device.

v0:
```python
import math
import jax
import jax.numpy as jnp
from jax import lax
from jax.sharding import PartitionSpec as P

HEAD_DIM = 128


def rotate(vectors, positions):
    half_dim = vectors.shape[-1] // 2
    frequency = 1000000.0 ** (-jnp.arange(half_dim, dtype=jnp.float32) / half_dim)
    angles = positions.astype(jnp.float32)[:, None, None] * frequency[None, None, :]
    cosine = jnp.cos(angles)
    sine_part = jnp.sin(angles)
    lower_half = vectors[..., :half_dim]
    upper_half = vectors[..., half_dim:]
    return jnp.concatenate(
        [
            lower_half * cosine - upper_half * sine_part,
            upper_half * cosine + lower_half * sine_part,
        ],
        axis=-1,
    )


def sum_hidden(partial_value):
    return lax.psum_scatter(partial_value, "tp", scatter_dimension=1, tiled=True).astype(
        jnp.bfloat16
    )


def project_strips(merger_hidden, merger_out):
    return jnp.dot(
        lax.all_gather(merger_hidden, ("role", "seq"), axis=0, tiled=True),
        merger_out,
        preferred_element_type=jnp.float32,
    )


def body(
    merger_hidden,
    merger_out,
    row_position,
    prompt_embeds,
    norm_gain,
    query_weight,
    key_weight,
    value_weight,
):
    groups = lax.axis_size("role") * lax.axis_size("seq")
    device_rank = lax.axis_index(("role", "seq"))
    row_count = merger_hidden.shape[0]
    tok_count = prompt_embeds.shape[0]
    columns = prompt_embeds.shape[1]
    model_width = columns * lax.axis_size("tp")
    capacity = 2 * row_count // groups
    strips = project_strips(merger_hidden, merger_out)
    partial_value = lax.all_to_all(strips, ("role", "seq"), split_axis=0, concat_axis=1, tiled=True)
    embeds = sum_hidden(partial_value)
    owners = jnp.where(row_position >= 0, row_position // tok_count, groups)
    onehot = (owners[:, None] == jnp.arange(groups, dtype=jnp.int32)[None, :]).astype(jnp.int32)
    earlier = jnp.sum((jnp.cumsum(onehot, axis=0) - onehot) * onehot, axis=1)
    buffer_slot = jnp.where(owners < groups, owners * capacity + earlier, groups * capacity)
    source = (
        jnp.full((groups * capacity,), row_count, jnp.int32)
        .at[buffer_slot]
        .set(jnp.arange(row_count, dtype=jnp.int32), mode="drop")
    )
    padded = jnp.concatenate([embeds, jnp.zeros((1, columns), jnp.bfloat16)], axis=0)
    outgoing = padded[source].reshape(groups, capacity, columns)
    outgoing_pos = jnp.concatenate([row_position, jnp.full((1,), -1, jnp.int32)])[source].reshape(
        groups, capacity
    )
    arrived, arrived_pos = (
        lax.all_to_all(outgoing, ("role", "seq"), split_axis=0, concat_axis=0, tiled=True),
        lax.all_to_all(outgoing_pos, ("role", "seq"), split_axis=0, concat_axis=0, tiled=True),
    )
    arrived_pos = arrived_pos.reshape(-1)
    local_row = jnp.where(arrived_pos >= 0, arrived_pos - device_rank * tok_count, tok_count)
    stream = prompt_embeds.at[local_row].set(arrived.reshape(-1, columns), mode="drop")
    widened = stream.astype(jnp.float32)
    squares = lax.psum(jnp.sum(widened * widened, axis=1), "tp")
    inverse = lax.rsqrt(squares / model_width + 1e-06)[:, None]
    normed = (widened * inverse * norm_gain.astype(jnp.float32)[None, :]).astype(jnp.bfloat16)
    tables = (query_weight, key_weight, value_weight)
    shard_piece = lax.all_gather(normed, "tp", axis=1, tiled=True)
    query_sum, key_sum, value_sum = tuple(
        (jnp.dot(shard_piece, table, preferred_element_type=jnp.float32) for table in tables)
    )
    local_heads = query_weight.shape[1] // HEAD_DIM
    local_kv = key_weight.shape[1] // HEAD_DIM
    group_size = local_heads // local_kv
    positions = device_rank * tok_count + jnp.arange(tok_count, dtype=jnp.int32)
    queries = rotate(query_sum.reshape(tok_count, local_heads, HEAD_DIM), positions).astype(
        jnp.bfloat16
    )
    queries = queries.reshape(tok_count, local_kv, group_size, HEAD_DIM)
    key_rows = rotate(key_sum.reshape(tok_count, local_kv, HEAD_DIM), positions).astype(
        jnp.bfloat16
    )
    value_rows = value_sum.astype(jnp.bfloat16).reshape(tok_count, local_kv, HEAD_DIM)
    score_scale = 1.0 / math.sqrt(HEAD_DIM)
    running_max = jnp.full((local_kv, group_size, tok_count), -1e30, jnp.float32)
    key_piece = lax.all_gather(key_rows, ("role", "seq"), axis=0, tiled=True)
    value_piece = lax.all_gather(value_rows, ("role", "seq"), axis=0, tiled=True)
    scores = (
        jnp.einsum("qhgd,khd->hgqk", queries, key_piece, preferred_element_type=jnp.float32)
        * score_scale
    )
    key_pos = jnp.arange(key_piece.shape[0], dtype=jnp.int32)
    visible = key_pos[None, :] <= positions[:, None]
    scores = jnp.where(visible, scores, -jnp.inf)
    next_max = jnp.maximum(running_max, jnp.max(scores, axis=3))
    probability = jnp.where(visible, jnp.exp(scores - next_max[..., None]), 0.0)
    running_sum = jnp.sum(probability, axis=3)
    running_out = jnp.einsum(
        "hgqk,khd->hgqd",
        probability.astype(jnp.bfloat16),
        value_piece,
        preferred_element_type=jnp.float32,
    )
    running_max, running_sum, running_out = (next_max, running_sum, running_out)
    context = running_out / running_sum[..., None]
    context = (
        jnp.transpose(context, (2, 0, 1, 3))
        .reshape(tok_count, local_heads * HEAD_DIM)
        .astype(jnp.bfloat16)
    )
    return (stream, context)


def solution(mesh):
    in_specs = (
        P(("role", "seq"), "tp"),
        P("tp", ("role", "seq")),
        P(("role", "seq")),
        P(("role", "seq"), "tp"),
        P("tp"),
        P(None, "tp"),
        P(None, "tp"),
        P(None, "tp"),
    )
    out_specs = (P(("role", "seq"), "tp"), P(("role", "seq"), "tp"))
    return jax.shard_map(body, mesh=mesh, in_specs=in_specs, out_specs=out_specs, check_vma=False)
```

profile of v0, /device:TPU:0, one launch (start us, length us, event | category | flops | bytes accessed | tf_op | source)
XLA Modules:
  0.0 304.1 jit_solution(15773914192989135023)
XLA Ops:
  7.2 2.5 copy.45
  9.8 26.2 %all-gather.4.cloned.1.call-done = bf16[512,1280]{1,0:T(8,128)(2,1)} async-done(((bf16[64,1280]{1,0:T(8,128)(2,1)}), bf16[512,1280]{1,0:T(8,128)(2,1)}) %all-gather.4.cloned.1.call-update) | async-done | bytes 1310736 | tf_op jit(solution)/shard_map/all_gather | solution.py:35
  36.0 2.8 fusion.37
  38.8 51.7 %all_to_all.33 = f32[8,64,1024]{2,1,0:T(8,128)S(1)} all-to-all(f32[8,64,1024]{2,1,0:T(8,128)S(1)} %bitcast.65), channel_id=1, replica_groups=mesh['role'=2,'seq'=4,'tp'=4] {'role','seq'}, dimensions={0} | all-to-all | bytes 4194304 | tf_op jit(solution)/shard_map/all_to_all | solution.py:59
  90.5 1.5 copy.37
  92.5 0.8 scatter_custom_fusion
  93.3 1.2 gather_fusion
  94.6 0.7 all_to_all.23
  95.2 3.3 %all-to-all-start = ((s32[8,1,16]{2,1,0:T(1,128)}), s32[8,1,16]{2,1,0:T(1,128)S(1)}, u32[]{:S(2)}, u32[]{:S(2)}) async-start(s32[8,1,16]{2,1,0:T(1,128)} %bitcast), calls=%async_computation | async-start | bytes 8192 | tf_op jit(solution)/shard_map/all_to_all | solution.py:77
  98.5 27.3 %reduce-scatter.2.cloned.1.call-done = f32[64,2048]{1,0:T(8,128)} async-done(((f32[64,8192]{1,0:T(8,128)}), f32[64,2048]{1,0:T(8,128)}) %reduce-scatter.2.cloned.1.call-update) | async-done | bytes 524304 | tf_op jit(solution)/shard_map/reduce_scatter | solution.py:28
  125.9 1.1 convert_element_type.54
  127.0 1.7 gather_fusion.1
  128.7 4.6 %all-to-all-start.2 = ((bf16[8,16,2048]{2,1,0:T(8,128)(2,1)}), bf16[8,16,2048]{2,1,0:T(8,128)(2,1)S(1)}, u32[]{:S(2)}, u32[]{:S(2)}) async-start(bf16[8,16,2048]{2,1,0:T(8,128)(2,1)} %bitcast.4), calls=%async_computation.3 | async-start | bytes 1048576 | tf_op jit(solution)/shard_map/all_to_all | solution.py:76
  133.5 14.6 %all-to-all-done.2 = bf16[8,16,2048]{2,1,0:T(8,128)(2,1)S(1)} async-done(((bf16[8,16,2048]{2,1,0:T(8,128)(2,1)}), bf16[8,16,2048]{2,1,0:T(8,128)(2,1)S(1)}, u32[]{:S(2)}, u32[]{:S(2)}) %all-to-all-start.2) | async-done | bytes 524320 | tf_op jit(solution)/shard_map/all_to_all | solution.py:76
  148.0 3.7 %scatter_fusion = bf16[256,2048]{1,0:T(8,128)(2,1)} fusion(bf16[256,2048]{1,0:T(8,128)(2,1)} %copy.45, s32[128]{0:T(128)S(1)} %fusion.28, bf16[128,2048]{1,0:T(8,128)(2,1)S(1)} %bitcast.64), kind=kCustom, calls=%fused_computation.3 | custom fusion | bytes 1573376 | tf_op jit(solution)/shard_map/scatter | solution.py:81
  151.7 1.5 fusion.7
  153.2 8.9 %psum.7 = f32[256]{0:T(256)S(1)} all-reduce(f32[256]{0:T(256)S(1)} %fusion.7), channel_id=1, replica_groups=mesh['role'=2,'seq'=4,'tp'=4] {'tp'}, use_global_device_ids=true, to_apply=%region_6.7 | all-reduce | flops 256 | bytes 2048 | tf_op jit(solution)/shard_map/psum | solution.py:83
  162.2 2.5 fusion.9
  164.7 0.5 multiply_cosine_fusion
  165.3 0.3 iota_compare_fusion
  165.6 49.5 %all-gather.6.cloned.1.call-done = bf16[256,8192]{1,0:T(8,128)(2,1)} async-done(((bf16[256,2048]{1,0:T(8,128)(2,1)}), bf16[256,8192]{1,0:T(8,128)(2,1)}) %all-gather.6.cloned.1.call-update) | async-done | bytes 4194320 | tf_op jit(solution)/shard_map/all_gather | solution.py:87
  215.1 4.5 %convolution_bitcast_fusion.1 = f32[256,1,128]{0,2,1:T(8,128)S(1)} fusion(bf16[256,8192]{1,0:T(8,128)(2,1)} %all-gather.6.cloned.1.call-done, bf16[8192,128]{1,0:T(8,128)(2,1)} %param.14), kind=kOutput, calls=%fused_computation.19 | convolution fusion | flops 536870912 | bytes 6422528 | tf_op jit(solution)/shard_map/dot_general | solution.py:89
  219.9 8.4 %convolution_bitcast_fusion = f32[32,8,8,128]{3,1,2,0:T(8,128)S(1)} fusion(bf16[256,8192]{1,0:T(8,128)(2,1)S(1)} %copy-done.1, bf16[8192,1024]{1,0:T(8,128)(2,1)} %param.13), kind=kOutput, calls=%fused_computation.18 | convolution fusion | flops 4294967296 | bytes 22020096 | tf_op jit(solution)/shard_map/dot_general | solution.py:89
  228.6 26.5 %all_gather.14 = bf16[2048,1,128]{0,2,1:T(8,128)(2,1)S(1)} all-gather(bf16[256,1,128]{0,2,1:T(8,128)(2,1)S(1)} %pad_maximum_fusion), channel_id=1, replica_groups=mesh['role'=2,'seq'=4,'tp'=4] {'role','seq'}, dimensions={0}, use_global_device_ids=true | all-gather | bytes 589824 | tf_op jit(solution)/shard_map/all_gather | solution.py:105
  255.1 1.2 convolution_convert_fusion
  256.3 26.6 %all-gather = bf16[2048,128]{1,0:T(8,128)(2,1)S(1)} all-gather(bf16[256,128]{1,0:T(8,128)(2,1)S(1)} %convolution_convert_fusion), channel_id=2, replica_groups=mesh['role'=2,'seq'=4,'tp'=4] {'role','seq'}, dimensions={0}, use_global_device_ids=true | all-gather | bytes 589824 | tf_op jit(solution)/shard_map/all_gather | solution.py:106
  283.0 0.3 fusion.36
  283.3 0.4 subtract_convert_fusion
  283.7 2.8 fusion
  286.6 4.0 %fusion.1 = f32[8,256]{1,0:T(8,128)S(1)} fusion(f32[2048,256,8]{1,0,2:T(8,128)S(1)} %get-tuple-element.17, f32[8,256]{1,0:T(8,128)S(1)} %broadcast_maximum_fusion, pred[256,2048]{0,1:T(8,128)(4,1)S(1)} %iota_compare_fusion), kind=kLoop, calls=%fused_computation.7 | loop fusion | flops 20969472 | bytes 17317888 | tf_op jit(solution)/shard_map/reduce_sum | solution.py:116
  290.6 4.9 %divide_convert_fusion = bf16[8,256,128]{1,2,0:T(8,128)(2,1)} fusion(f32[2048,256,8]{1,0,2:T(8,128)S(1)} %get-tuple-element.17, f32[8,256]{1,0:T(8,128)S(1)} %broadcast_maximum_fusion, pred[256,2048]{0,1:T(8,128)(4,1)S(1)} %iota_compare_fusion, bf16[2048,128]{1,0:T(8,128)(2,1)S(1)} %all-gather, f32[8,256]{1,0:T(8,128)S(1)} %fusion.1), kind=kOutput, calls=%fused_computation.21 | convolution fusion | flops 1095237632 | bytes 18366464 | tf_op jit(solution)/shard_map/hgqk,khd->hgqd/dot_general | solution.py:117
  295.5 2.0 copy.29
  (39 shorter events, 1.3 us)
Async XLA Ops:
  7.2 28.8 %copy-start = (bf16[1280,1024]{1,0:T(8,128)(2,1)S(1)}, bf16[1280,1024]{1,0:T(8,128)(2,1)}, u32[]{:S(2)}) copy-start(bf16[1280,1024]{1,0:T(8,128)(2,1)} %param.9) | copy-start | bytes 7864324
  7.2 28.8 %all-gather.4.cloned.1.call-start = ((), (), s32[]{:S(2)}) async-start(), calls=%async_computation.4 | async-start | bytes 1474560 | tf_op jit(solution)/shard_map/all_gather | solution.py:35
  9.7 116.1 %reduce-scatter.2.cloned.1.call-start = ((), (), s32[]{:S(2)}) async-start(), calls=%async_computation.5 | async-start | bytes 2621440 | tf_op jit(solution)/shard_map/reduce_scatter | solution.py:28
  90.5 1.5 copy-start.4
  92.1 41.3 %copy-start.3 = (bf16[2048]{0:T(1024)(128)(2,1)S(1)}, bf16[2048]{0:T(1024)(128)(2,1)}, u32[]{:S(2)}) copy-start(bf16[2048]{0:T(1024)(128)(2,1)} %param.12) | copy-start | bytes 12292
  95.2 33.4 %all-to-all-start = ((s32[8,1,16]{2,1,0:T(1,128)}), s32[8,1,16]{2,1,0:T(1,128)S(1)}, u32[]{:S(2)}, u32[]{:S(2)}) async-start(s32[8,1,16]{2,1,0:T(1,128)} %bitcast), calls=%async_computation | async-start | bytes 8192 | tf_op jit(solution)/shard_map/all_to_all | solution.py:77
  128.7 19.4 %all-to-all-start.2 = ((bf16[8,16,2048]{2,1,0:T(8,128)(2,1)}), bf16[8,16,2048]{2,1,0:T(8,128)(2,1)S(1)}, u32[]{:S(2)}, u32[]{:S(2)}) async-start(bf16[8,16,2048]{2,1,0:T(8,128)(2,1)} %bitcast.4), calls=%async_computation.3 | async-start | bytes 1048576 | tf_op jit(solution)/shard_map/all_to_all | solution.py:76
  133.3 81.8 %all-gather.6.cloned.1.call-start = ((), (), s32[]{:S(2)}) async-start(), calls=%async_computation.6 | async-start | bytes 5242880 | tf_op jit(solution)/shard_map/all_gather | solution.py:87
  215.1 4.8 %copy-start.1 = (bf16[256,8192]{1,0:T(8,128)(2,1)S(1)}, bf16[256,8192]{1,0:T(8,128)(2,1)}, u32[]{:S(2)}) copy-start(bf16[256,8192]{1,0:T(8,128)(2,1)} %all-gather.6.cloned.1.call-done) | copy-start | bytes 12582916
  219.9 35.2 %copy-start.2 = (bf16[8192,128]{1,0:T(8,128)(2,1)S(1)}, bf16[8192,128]{1,0:T(8,128)(2,1)}, u32[]{:S(2)}) copy-start(bf16[8192,128]{1,0:T(8,128)(2,1)} %param.15) | copy-start | bytes 6291460
Sparse Core Ops, SparseCore 0:
  9.8 26.1 all-gather.3
  92.2 33.6 reduce-scatter.1
  164.8 50.2 all-gather.5
where the time goes:
time: 305 us; the launch traced here: 304 us
  waiting for transfers between devices  118 us (39%)
  blocking collectives  114 us (37%)
  matrix products  24.7 us (8%)
  local copies, waits for them, and re-layouts  14.7 us (5%)
  between operations  14 us (5%)
  other arithmetic  11.2 us (4%)
  starting transfers between devices  7.98 us (3%)
    all_to_all x1, blocking collectives, body(): lax.all_to_all(strips, ('role', 'seq'), split_axis=0, concat_axis=1, tile...  51.7 us
    all_gather x1, waiting for transfers between devices, body(): shard_piece = lax.all_gather(normed, 'tp', axis=1, tiled=True)  49.5 us
    reduce_scatter x1, waiting for transfers between devices, sum_hidden(): lax.psum_scatter(partial_value, 'tp', scatter_dimension=1, tiled=True)  27.3 us
    all_gather x1, blocking collectives, body(): lax.all_gather(value_rows, ('role', 'seq'), axis=0, tiled=True)  26.6 us
    all_gather x1, blocking collectives, body(): key_piece = lax.all_gather(key_rows, ('role', 'seq'), axis=0, tiled=True)  26.5 us
    all_gather x1, waiting for transfers between devices, project_strips(): lax.all_gather(merger_hidden, ('role', 'seq'), axis=0, tiled=True)  26.2 us
    all_to_all x1, waiting for transfers between devices, body(): lax.all_to_all(outgoing, ('role', 'seq'), split_axis=0, concat_axis=0, ti...  14.6 us
    dot_general x3, matrix products, body(): jnp.dot(shard_piece, table, preferred_element_type=jnp.float32)  14.2 us
  transfers between devices with their start and end apart: 5, of which 4 were waited for; matrix products, arithmetic and copies ran while one was open for 2% of the time, Pallas kernels for 0%

commit v1 on v0

--- a/solution.py
+++ b/solution.py
@@ -3,6 +3,7 @@
 import jax.numpy as jnp
 from jax import lax
 from jax.sharding import PartitionSpec as P
+from jax.lax import all_gather
 
 HEAD_DIM = 128
 
@@ -102,8 +103,11 @@
     value_rows = value_sum.astype(jnp.bfloat16).reshape(tok_count, local_kv, HEAD_DIM)
     score_scale = 1.0 / math.sqrt(HEAD_DIM)
     running_max = jnp.full((local_kv, group_size, tok_count), -1e30, jnp.float32)
-    key_piece = lax.all_gather(key_rows, ("role", "seq"), axis=0, tiled=True)
-    value_piece = lax.all_gather(value_rows, ("role", "seq"), axis=0, tiled=True)
+    key_piece, value_piece = jnp.split(
+        all_gather(jnp.concatenate([key_rows, value_rows], 1), ("role", "seq"), axis=0, tiled=True),
+        [key_rows.shape[1]],
+        axis=1,
+    )
     scores = (
         jnp.einsum("qhgd,khd->hgqk", queries, key_piece, preferred_element_type=jnp.float32)
         * score_scale

time: 305 us -> 269 us (0.88)
  blocking collectives: 114 us -> 60.6 us
  waiting for transfers between devices: 118 us -> 130 us
    all_gather x2 -> x0, blocking collectives: 53.1 us -> none  [the longest x1 26.6 us: body(): lax.all_gather(value_rows, ('role', 'seq'), axis=0, tiled=True)]
    all_gather x0 -> x1, waiting for transfers between devices: none -> 12.7 us  [body(): all_gather(jnp.concatenate([key_rows, value_rows], 1), ('role', 'seq'), a...]
  transfers between devices with their start and end apart: 5 -> 6, of which waited for: 4 -> 5; matrix products, arithmetic and copies ran while one was open for 2% -> 7% of each run, Pallas kernels for 0% -> 0%
where the time goes in v1:
time: 269 us; the launch traced here: 268 us
  waiting for transfers between devices  130 us (48%)
  blocking collectives  60.6 us (23%)
  matrix products  27.5 us (10%)
  local copies, waits for them, and re-layouts  14.7 us (5%)
  between operations  14 us (5%)
  other arithmetic  12.9 us (5%)
  starting transfers between devices  8.21 us (3%)
    all_to_all x1, blocking collectives, body(): lax.all_to_all(strips, ('role', 'seq'), split_axis=0, concat_axis=1, tile...  51.7 us
    all_gather x1, waiting for transfers between devices, body(): shard_piece = lax.all_gather(normed, 'tp', axis=1, tiled=True)  49.2 us
    reduce_scatter x1, waiting for transfers between devices, sum_hidden(): lax.psum_scatter(partial_value, 'tp', scatter_dimension=1, tiled=True)  27.3 us
    all_gather x1, waiting for transfers between devices, project_strips(): lax.all_gather(merger_hidden, ('role', 'seq'), axis=0, tiled=True)  26.2 us
    dot_general x3, matrix products, body(): jnp.dot(shard_piece, table, preferred_element_type=jnp.float32)  15.4 us
    all_to_all x1, waiting for transfers between devices, body(): lax.all_to_all(outgoing, ('role', 'seq'), split_axis=0, concat_axis=0, ti...  14.6 us
    all_gather x1, waiting for transfers between devices, body(): all_gather(jnp.concatenate([key_rows, value_rows], 1), ('role', 'seq'), a...  12.7 us
    psum x1, blocking collectives, body(): squares = lax.psum(jnp.sum(widened * widened, axis=1), 'tp')  8.93 us
  transfers between devices with their start and end apart: 6, of which 5 were waited for; matrix products, arithmetic and copies ran while one was open for 7% of the time, Pallas kernels for 0%

profile of v1, /device:TPU:0, one launch (start us, length us, event | category | flops | bytes accessed | tf_op | source)
XLA Modules:
  0.0 268.1 jit_solution(10362647996271629054)
XLA Ops:
  7.2 2.5 copy.46
  9.8 26.2 %all-gather.4.cloned.1.call-done = bf16[512,1280]{1,0:T(8,128)(2,1)} async-done(((bf16[64,1280]{1,0:T(8,128)(2,1)}), bf16[512,1280]{1,0:T(8,128)(2,1)}) %all-gather.4.cloned.1.call-update) | async-done | bytes 1310736 | tf_op jit(solution)/shard_map/all_gather | solution.py:36
  36.0 2.8 %fusion.36 = f32[512,1024]{1,0:T(8,128)S(1)} fusion(bf16[512,1280]{1,0:T(8,128)(2,1)} %all-gather.4.cloned.1.call-done, bf16[1280,1024]{1,0:T(8,128)(2,1)S(1)} %copy-done), kind=kOutput, calls=%fused_computation.73 | convolution fusion | flops 1342177280 | bytes 6029312 | tf_op jit(solution)/shard_map/dot_general | solution.py:35
  38.8 51.7 %all_to_all.33 = f32[8,64,1024]{2,1,0:T(8,128)S(1)} all-to-all(f32[8,64,1024]{2,1,0:T(8,128)S(1)} %bitcast.68), channel_id=1, replica_groups=mesh['role'=2,'seq'=4,'tp'=4] {'role','seq'}, dimensions={0} | all-to-all | bytes 4194304 | tf_op jit(solution)/shard_map/all_to_all | solution.py:60
  90.5 1.5 copy.38
  92.5 0.8 scatter_custom_fusion
  93.3 1.2 gather_fusion
  94.6 0.7 all_to_all.23
  95.2 3.3 %all-to-all-start = ((s32[8,1,16]{2,1,0:T(1,128)}), s32[8,1,16]{2,1,0:T(1,128)S(1)}, u32[]{:S(2)}, u32[]{:S(2)}) async-start(s32[8,1,16]{2,1,0:T(1,128)} %bitcast), calls=%async_computation | async-start | bytes 8192 | tf_op jit(solution)/shard_map/all_to_all | solution.py:78
  98.5 27.3 %reduce-scatter.2.cloned.1.call-done = f32[64,2048]{1,0:T(8,128)} async-done(((f32[64,8192]{1,0:T(8,128)}), f32[64,2048]{1,0:T(8,128)}) %reduce-scatter.2.cloned.1.call-update) | async-done | bytes 524304 | tf_op jit(solution)/shard_map/reduce_scatter | solution.py:29
  125.9 1.1 convert_element_type.54
  127.0 1.7 gather_fusion.1
  128.7 4.6 %all-to-all-start.2 = ((bf16[8,16,2048]{2,1,0:T(8,128)(2,1)}), bf16[8,16,2048]{2,1,0:T(8,128)(2,1)S(1)}, u32[]{:S(2)}, u32[]{:S(2)}) async-start(bf16[8,16,2048]{2,1,0:T(8,128)(2,1)} %bitcast.4), calls=%async_computation.3 | async-start | bytes 1048576 | tf_op jit(solution)/shard_map/all_to_all | solution.py:77
  133.5 14.6 %all-to-all-done.2 = bf16[8,16,2048]{2,1,0:T(8,128)(2,1)S(1)} async-done(((bf16[8,16,2048]{2,1,0:T(8,128)(2,1)}), bf16[8,16,2048]{2,1,0:T(8,128)(2,1)S(1)}, u32[]{:S(2)}, u32[]{:S(2)}) %all-to-all-start.2) | async-done | bytes 524320 | tf_op jit(solution)/shard_map/all_to_all | solution.py:77
  148.0 3.7 %scatter_fusion = bf16[256,2048]{1,0:T(8,128)(2,1)} fusion(bf16[256,2048]{1,0:T(8,128)(2,1)} %copy.46, s32[128]{0:T(128)S(1)} %fusion.27, bf16[128,2048]{1,0:T(8,128)(2,1)S(1)} %bitcast.67), kind=kCustom, calls=%fused_computation.3 | custom fusion | bytes 1573376 | tf_op jit(solution)/shard_map/scatter | solution.py:82
  151.7 1.5 fusion.7
  153.2 8.9 %psum.7 = f32[256]{0:T(256)S(1)} all-reduce(f32[256]{0:T(256)S(1)} %fusion.7), channel_id=1, replica_groups=mesh['role'=2,'seq'=4,'tp'=4] {'tp'}, use_global_device_ids=true, to_apply=%region_6.7 | all-reduce | flops 256 | bytes 2048 | tf_op jit(solution)/shard_map/psum | solution.py:84
  162.2 2.5 fusion.9
  165.0 0.5 multiply_cosine_fusion
  165.5 0.3 iota_compare_fusion
  165.8 49.2 %all-gather.6.cloned.1.call-done = bf16[256,8192]{1,0:T(8,128)(2,1)} async-done(((bf16[256,2048]{1,0:T(8,128)(2,1)}), bf16[256,8192]{1,0:T(8,128)(2,1)}) %all-gather.6.cloned.1.call-update) | async-done | bytes 4194320 | tf_op jit(solution)/shard_map/all_gather | solution.py:88
  215.1 4.5 %convolution_bitcast_fusion.1 = f32[256,1,128]{0,2,1:T(8,128)S(1)} fusion(bf16[256,8192]{1,0:T(8,128)(2,1)} %all-gather.6.cloned.1.call-done, bf16[8192,128]{1,0:T(8,128)(2,1)} %param.14), kind=kOutput, calls=%fused_computation.19 | convolution fusion | flops 536870912 | bytes 6422528 | tf_op jit(solution)/shard_map/dot_general | solution.py:90
  219.9 1.5 fusion.10
  221.5 0.6 pad_maximum_fusion
  222.1 9.4 %convolution_bitcast_fusion = f32[32,8,8,128]{3,1,2,0:T(8,128)S(1)} fusion(bf16[256,8192]{1,0:T(8,128)(2,1)} %all-gather.6.cloned.1.call-done, bf16[8192,1024]{1,0:T(8,128)(2,1)} %param.13), kind=kOutput, calls=%fused_computation.18 | convolution fusion | flops 4294967296 | bytes 22020096 | tf_op jit(solution)/shard_map/dot_general | solution.py:90
  231.8 0.3 fusion.35
  232.1 1.4 subtract_convert_fusion
  233.5 12.7 %all-gather.8.cloned.1.call-done = bf16[2048,2,128]{0,2,1:T(8,128)(2,1)} async-done(((bf16[256,2,128]{0,2,1:T(8,128)(2,1)}), bf16[2048,2,128]{0,2,1:T(8,128)(2,1)}) %all-gather.8.cloned.1.call-update) | async-done | bytes 1048592 | tf_op jit(solution)/shard_map/all_gather | solution.py:107
  246.2 4.2 %fusion = (f32[8,256]{1,0:T(8,128)S(1)}, f32[2048,256,8]{1,0,2:T(8,128)S(1)}) fusion(pred[256,2048]{0,1:T(8,128)(4,1)S(1)} %iota_compare_fusion, bf16[256,8,64]{2,0,1:T(8,128)(2,1)} %get-tuple-element.9, bf16[256,8,64]{2,0,1:T(8,128)(2,1)} %get-tuple-element.8, bf16[2048,2,128]{0,2,1:T(8,128)(2,1)} %all-gather.8.cloned.1.call-done), kind=kOutput, calls=%fused_computation.6 | convolution fusion | flops 1087371264 | bytes 18882560 | tf_op jit(solution)/shard_map/qhgd,khd->hgqk/dot_general | solution.py:112
  250.5 4.0 %fusion.1 = f32[8,256]{1,0:T(8,128)S(1)} fusion(f32[2048,256,8]{1,0,2:T(8,128)S(1)} %get-tuple-element.17, f32[8,256]{1,0:T(8,128)S(1)} %broadcast_maximum_fusion, pred[256,2048]{0,1:T(8,128)(4,1)S(1)} %iota_compare_fusion), kind=kLoop, calls=%fused_computation.7 | loop fusion | flops 20969472 | bytes 17317888 | tf_op jit(solution)/shard_map/reduce_sum | solution.py:120
  254.5 5.0 %divide_convert_fusion = bf16[8,256,128]{1,2,0:T(8,128)(2,1)} fusion(f32[2048,256,8]{1,0,2:T(8,128)S(1)} %get-tuple-element.17, f32[8,256]{1,0:T(8,128)S(1)} %broadcast_maximum_fusion, pred[256,2048]{0,1:T(8,128)(4,1)S(1)} %iota_compare_fusion, bf16[2048,2,128]{0,2,1:T(8,128)(2,1)S(1)} %copy-done.3, f32[8,256]{1,0:T(8,128)S(1)} %fusion.1), kind=kOutput, calls=%fused_computation.22 | convolution fusion | flops 1095237632 | bytes 18366464 | tf_op jit(solution)/shard_map/hgqk,khd->hgqd/dot_general | solution.py:121
  259.5 2.0 copy.31
  (42 shorter events, 1.6 us)
Async XLA Ops:
  7.2 28.8 %copy-start = (bf16[1280,1024]{1,0:T(8,128)(2,1)S(1)}, bf16[1280,1024]{1,0:T(8,128)(2,1)}, u32[]{:S(2)}) copy-start(bf16[1280,1024]{1,0:T(8,128)(2,1)} %param.9) | copy-start | bytes 7864324
  7.2 28.8 %all-gather.4.cloned.1.call-start = ((), (), s32[]{:S(2)}) async-start(), calls=%async_computation.4 | async-start | bytes 1474560 | tf_op jit(solution)/shard_map/all_gather | solution.py:36
  9.7 116.1 %reduce-scatter.2.cloned.1.call-start = ((), (), s32[]{:S(2)}) async-start(), calls=%async_computation.5 | async-start | bytes 2621440 | tf_op jit(solution)/shard_map/reduce_scatter | solution.py:29
  90.5 1.5 copy-start.5
  92.1 41.3 %copy-start.4 = (bf16[2048]{0:T(1024)(128)(2,1)S(1)}, bf16[2048]{0:T(1024)(128)(2,1)}, u32[]{:S(2)}) copy-start(bf16[2048]{0:T(1024)(128)(2,1)} %param.12) | copy-start | bytes 12292
  95.2 33.4 %all-to-all-start = ((s32[8,1,16]{2,1,0:T(1,128)}), s32[8,1,16]{2,1,0:T(1,128)S(1)}, u32[]{:S(2)}, u32[]{:S(2)}) async-start(s32[8,1,16]{2,1,0:T(1,128)} %bitcast), calls=%async_computation | async-start | bytes 8192 | tf_op jit(solution)/shard_map/all_to_all | solution.py:78
  128.7 19.4 %all-to-all-start.2 = ((bf16[8,16,2048]{2,1,0:T(8,128)(2,1)}), bf16[8,16,2048]{2,1,0:T(8,128)(2,1)S(1)}, u32[]{:S(2)}, u32[]{:S(2)}) async-start(bf16[8,16,2048]{2,1,0:T(8,128)(2,1)} %bitcast.4), calls=%async_computation.3 | async-start | bytes 1048576 | tf_op jit(solution)/shard_map/all_to_all | solution.py:77
  133.3 81.8 %all-gather.6.cloned.1.call-start = ((), (), s32[]{:S(2)}) async-start(), calls=%async_computation.6 | async-start | bytes 5242880 | tf_op jit(solution)/shard_map/all_gather | solution.py:88
  164.7 81.5 %all-gather.8.cloned.1.call-start = ((), (), s32[]{:S(2)}) async-start(), calls=%async_computation.7 | async-start | bytes 1179648 | tf_op jit(solution)/shard_map/all_gather | solution.py:107
  215.1 4.8 %copy-start.1 = (bf16[256,8192]{1,0:T(8,128)(2,1)S(1)}, bf16[256,8192]{1,0:T(8,128)(2,1)}, u32[]{:S(2)}) copy-start(bf16[256,8192]{1,0:T(8,128)(2,1)} %all-gather.6.cloned.1.call-done) | copy-start | bytes 12582916
  215.1 4.8 %copy-start.2 = (bf16[8192,128]{1,0:T(8,128)(2,1)S(1)}, bf16[8192,128]{1,0:T(8,128)(2,1)}, u32[]{:S(2)}) copy-start(bf16[8192,128]{1,0:T(8,128)(2,1)} %param.15) | copy-start | bytes 6291460
  250.4 4.0 %copy-start.3 = (bf16[2048,2,128]{0,2,1:T(8,128)(2,1)S(1)}, bf16[2048,2,128]{0,2,1:T(8,128)(2,1)}, u32[]{:S(2)}) copy-start(bf16[2048,2,128]{0,2,1:T(8,128)(2,1)} %all-gather.8.cloned.1.call-done) | copy-start | bytes 3145732
Sparse Core Ops, SparseCore 0:
  9.8 26.1 all-gather.3
  92.2 33.6 reduce-scatter.1
  164.8 50.2 all-gather.5
  222.3 23.8 all-gather.7
